TPU v7x, 32 devices: a whole 2x2x4 slice. The times are simulated.
32 devices in a mesh: panel: 2 (over y), row: 4 (over z), layer: 4 (over x, core).
Axes of the slice: x: 2, y: 2, z: 4, core: 2. Of those that a mesh axis runs over, the one named last changes fastest.
Arguments:
- layers: bfloat16 [4, 8192, 512], P('layer', 'row', 'panel'), parts along dimension 2, may hold values from -6 to 6
- table: bfloat16 [16, 128, 64], replicated, may hold values from -0.375 to 0.375
- fitting: bfloat16 [8192, 6600], P('row', 'layer'), may hold values from -0.09375 to 0.09375
- owner: int32 [4, 128, 1], P('layer', 'row'), may hold values from 0 to 3; in each aligned block of 32 rows (0 to 31, 32 to 63, ..., all dimensions but the last counted through in order) at most 16 rows name the same one
- local_slice: int32 [4, 128], P('layer', 'row'), may hold values from 0 to 15
- block_index: int32 [4, 128], P('layer', 'row'), may hold values from 0 to 31
- weight_index: int32 [4, 128], P('layer', 'row'), may hold values from 0 to 15
Outputs:
- actuators: bfloat16 [512, 6600], P(('panel', 'row'), 'layer'), parts along dimension 0
There are 2 independent parts, one for each index of `panel`. A program takes and returns all parts, laid end to end along the dimension named above; an argument that names none is the same for every part. Nothing has to cross between parts.
Inputs may be any that keep to these rules, and one draw needn't show every extreme that they name: `owner`: within the 32 entries of one layer on one row device (aligned blocks of 32 entries), no value is named more than 16 times, and in every draw some block names one value exactly 16 times.
All inputs are finite; a program needn't handle non-finite values.
Results may differ from a plain program's by a relative error of at most 0.0058.
Values may be sent and summed in bfloat16 or wider, within the bound.
A program may use at most 64 MiB of HBM per device.

v0:
```python
import jax
import jax.numpy as jnp
from jax import lax
from jax.sharding import PartitionSpec as P


def local(layers, table, fitting, owner, local_slice, block_index, weight_index):
    rows_dev = layers.shape[1]
    columns = layers.shape[2]
    slice_rows = table.shape[1]
    block_rows = table.shape[2]
    entries = owner.shape[1]
    peer_count = lax.axis_size("row")
    capacity = max(2, 2 * entries // peer_count)
    slot_count = peer_count * capacity
    owned_slices = fitting.shape[0] // slice_rows
    owner_now = owner[0, :, 0]
    local_now = local_slice[0]
    owner_match = (owner_now[:, None] == jnp.arange(peer_count, dtype=jnp.int32)[None, :]).astype(
        jnp.int32
    )
    slot_rank = jnp.sum((jnp.cumsum(owner_match, axis=0) - 1) * owner_match, axis=1)
    target = owner_now * capacity + slot_rank
    placed = target[None, :] == jnp.arange(slot_count, dtype=jnp.int32)[:, None]
    filled = jnp.any(placed, axis=1)
    source = jnp.sum(jnp.where(placed, jnp.arange(entries, dtype=jnp.int32)[None, :], 0), axis=1)
    send_local = jnp.where(filled, local_now[source], -1).reshape(peer_count, capacity)
    grouped = layers[0].reshape(rows_dev // block_rows, block_rows, columns)
    picked = grouped[block_index[0][source]].reshape(peer_count, capacity, block_rows, columns)
    send_weight = weight_index[0][source].reshape(peer_count, capacity)
    got_rows, got_weight, got_local = (
        lax.all_to_all(picked, "row", split_axis=0, concat_axis=0, tiled=True),
        lax.all_to_all(send_weight, "row", split_axis=0, concat_axis=0, tiled=True),
        lax.all_to_all(send_local, "row", split_axis=0, concat_axis=0, tiled=True),
    )
    pupil_terms = jnp.einsum(
        "ksb,kbc->ksc",
        table[got_weight.reshape(-1)],
        got_rows.reshape(slot_count, block_rows, columns),
        preferred_element_type=jnp.float32,
    ).astype(jnp.bfloat16)
    selector = (
        jnp.arange(owned_slices, dtype=jnp.int32)[:, None] == got_local.reshape(-1)[None, :]
    ).astype(jnp.bfloat16)
    partial_pupil = jnp.dot(
        selector,
        pupil_terms.reshape(slot_count, slice_rows * columns),
        preferred_element_type=jnp.float32,
    ).reshape(owned_slices * slice_rows, columns)
    pupil_rounded = lax.psum(partial_pupil, "layer").astype(jnp.bfloat16)
    return lax.psum_scatter(
        lax.dot_general(
            pupil_rounded, fitting, (((0,), (0,)), ((), ())), preferred_element_type=jnp.float32
        ),
        "row",
        scatter_dimension=0,
        tiled=True,
    ).astype(jnp.bfloat16)


def solution(mesh):
    return jax.shard_map(
        local,
        mesh=mesh,
        in_specs=(
            P("layer", "row", "panel"),
            P(),
            P("row", "layer"),
            P("layer", "row", None),
            P("layer", "row"),
            P("layer", "row"),
            P("layer", "row"),
        ),
        out_specs=P(("panel", "row"), "layer"),
        check_vma=False,
    )
```

profile of v0, /device:TPU:0, one launch (start us, length us, event | category | flops | bytes accessed | tf_op | source)
XLA Modules:
  0.0 183.3 jit_solution(12246338649943333909)
XLA Ops:
  6.5 0.0 copy-start
  6.5 0.8 fusion.3
  7.4 0.1 reduce_window_sum.11
  7.4 0.8 select_reduce_fusion.1
  8.2 0.7 multiply_add_fusion
  8.9 0.1 select_reduce_fusion
  9.0 1.4 gather_fusion.1
  10.4 0.7 all_to_all.14
  11.1 6.3 %all-to-all-start.1 = ((s32[4,1,16]{2,1,0:T(1,128)}), s32[4,1,16]{2,1,0:T(1,128)S(1)}, u32[]{:S(2)}, u32[]{:S(2)}) async-start(s32[4,1,16]{2,1,0:T(1,128)} %bitcast.6), calls=%async_computation.1 | async-start | bytes 4096 | tf_op jit(solution)/shard_map/all_to_all | solution.py:33
  17.5 0.1 fusion.2
  17.6 1.4 gather_fusion.3
  19.0 1.4 gather_fusion
  20.4 0.7 select_n.54
  21.1 1.8 %all-to-all-done.1 = s32[4,1,16]{2,1,0:T(1,128)S(1)} async-done(((s32[4,1,16]{2,1,0:T(1,128)}), s32[4,1,16]{2,1,0:T(1,128)S(1)}, u32[]{:S(2)}, u32[]{:S(2)}) %all-to-all-start.1) | async-done | bytes 288 | tf_op jit(solution)/shard_map/all_to_all | solution.py:33
  23.0 3.2 %all-to-all-start = ((s32[4,1,16]{2,1,0:T(1,128)}), s32[4,1,16]{2,1,0:T(1,128)S(1)}, u32[]{:S(2)}, u32[]{:S(2)}) async-start(s32[4,1,16]{2,1,0:T(1,128)} %bitcast.4), calls=%async_computation | async-start | bytes 4096 | tf_op jit(solution)/shard_map/all_to_all | solution.py:34
  26.2 0.0 copy-done
  26.2 2.0 %gather_fusion.4 = bf16[64,64,256]{2,1,0:T(8,128)(2,1)} fusion(bf16[32,64,256]{2,1,0:T(8,128)(2,1)S(1)} %bitcast.27, s32[1024]{0:T(1024)S(1)} %pad_clamp_fusion), kind=kCustom, calls=%fused_computation.4 | custom fusion | bytes 4194560 | tf_op jit(solution)/shard_map/gather | solution.py:29
  28.3 3.5 %all-to-all-done = s32[4,1,16]{2,1,0:T(1,128)S(1)} async-done(((s32[4,1,16]{2,1,0:T(1,128)}), s32[4,1,16]{2,1,0:T(1,128)S(1)}, u32[]{:S(2)}, u32[]{:S(2)}) %all-to-all-start) | async-done | bytes 288 | tf_op jit(solution)/shard_map/all_to_all | solution.py:34
  31.8 0.0 copy-start.1
  31.8 4.6 %all-to-all-start.2 = ((bf16[4,16,64,256]{3,2,1,0:T(8,128)(2,1)}), bf16[4,16,64,256]{3,2,1,0:T(8,128)(2,1)}, u32[]{:S(2)}, u32[]{:S(2)}) async-start(bf16[4,16,64,256]{3,2,1,0:T(8,128)(2,1)} %bitcast.12), calls=%async_computation.2 | async-start | bytes 4194304 | tf_op jit(solution)/shard_map/all_to_all | solution.py:32
  36.4 0.0 reduce-scatter.2.cloned.1.call-start
  36.4 0.5 broadcast.101
  36.9 0.7 reduce.6
  37.6 0.1 reshape.109
  37.7 0.7 reduce.7
  38.4 0.1 eq.48
  38.5 0.0 copy-done.1
  38.5 0.7 gather_fusion.2
  39.2 43.5 %all-to-all-done.2 = bf16[4,16,64,256]{3,2,1,0:T(8,128)(2,1)} async-done(((bf16[4,16,64,256]{3,2,1,0:T(8,128)(2,1)}), bf16[4,16,64,256]{3,2,1,0:T(8,128)(2,1)}, u32[]{:S(2)}, u32[]{:S(2)}) %all-to-all-start.2) | async-done | bytes 2097184 | tf_op jit(solution)/shard_map/all_to_all | solution.py:32
  82.8 2.9 %convolution_convert_fusion = bf16[64,128,256]{2,1,0:T(8,128)(2,1)S(1)} fusion(bf16[64,128,64]{1,2,0:T(8,128)(2,1)S(1)} %gather_fusion.2, bf16[64,64,256]{2,1,0:T(8,128)(2,1)} %bitcast.13), kind=kOutput, calls=%fused_computation.5 | convolution fusion | flops 270532608 | bytes 7340032 | tf_op jit(solution)/shard_map/ksb,kbc->ksc/dot_general | solution.py:36
  85.7 2.6 %copy.12 = bf16[8,8,128,256]{3,1,2,0:T(8,128)(2,1)S(1)} copy(bf16[8,8,128,256]{3,2,1,0:T(8,128)(2,1)S(1)} %bitcast.31) | data formatting | bytes 8388608
  88.3 0.7 fusion.4
  89.0 1.5 reshape.113
  90.5 40.8 %all-reduce.1 = bf16[2048,256]{1,0:T(8,128)(2,1)S(1)} all-reduce(f32[2048,256]{1,0:T(8,128)} %reshape.113), channel_id=1, replica_groups=mesh['panel'=2,'row'=4,'layer'=4] {'layer'}, use_global_device_ids=true, to_apply=%region_4.5 | all-reduce | flops 524288 | bytes 3145728 | tf_op jit(solution)/shard_map/psum | solution.py:50
  131.3 6.2 %fusion.9 = f32[256,1650]{1,0:T(8,128)} fusion(bf16[2048,256]{1,0:T(8,128)(2,1)S(1)} %all-reduce.1, bf16[2048,1650]{0,1:T(8,128)(2,1)} %param.9), kind=kOutput, calls=%fused_computation.28 | convolution fusion | flops 1730150400 | bytes 9496576 | tf_op jit(solution)/shard_map/dot_general | solution.py:52
  137.5 0.0 reduce-scatter.2.cloned.1.call-update
  137.5 37.2 %reduce-scatter.2.cloned.1.call-done = f32[64,1650]{1,0:T(8,128)} async-done(((f32[256,1650]{1,0:T(8,128)}), f32[64,1650]{1,0:T(8,128)}) %reduce-scatter.2.cloned.1.call-update) | async-done | bytes 422416 | tf_op jit(solution)/shard_map/reduce_scatter | solution.py:51
  174.7 1.7 convert_element_type.16
  (7 shorter events, 0.0 us)
Async XLA Ops:
  6.5 19.7 %copy-start = (bf16[1,2048,256]{2,1,0:T(8,128)(2,1)S(1)}, bf16[1,2048,256]{2,1,0:T(8,128)(2,1)}, u32[]{:S(2)}) copy-start(bf16[1,2048,256]{2,1,0:T(8,128)(2,1)} %param.7) | copy-start | bytes 3145732
  11.1 11.8 %all-to-all-start.1 = ((s32[4,1,16]{2,1,0:T(1,128)}), s32[4,1,16]{2,1,0:T(1,128)S(1)}, u32[]{:S(2)}, u32[]{:S(2)}) async-start(s32[4,1,16]{2,1,0:T(1,128)} %bitcast.6), calls=%async_computation.1 | async-start | bytes 4096 | tf_op jit(solution)/shard_map/all_to_all | solution.py:33
  23.0 8.8 %all-to-all-start = ((s32[4,1,16]{2,1,0:T(1,128)}), s32[4,1,16]{2,1,0:T(1,128)S(1)}, u32[]{:S(2)}, u32[]{:S(2)}) async-start(s32[4,1,16]{2,1,0:T(1,128)} %bitcast.4), calls=%async_computation | async-start | bytes 4096 | tf_op jit(solution)/shard_map/all_to_all | solution.py:34
  31.8 6.7 %copy-start.1 = (bf16[16,128,64]{1,2,0:T(8,128)(2,1)S(1)}, bf16[16,128,64]{1,2,0:T(8,128)(2,1)}, u32[]{:S(2)}) copy-start(bf16[16,128,64]{1,2,0:T(8,128)(2,1)} %param.8) | copy-start | bytes 786436
  31.8 51.0 %all-to-all-start.2 = ((bf16[4,16,64,256]{3,2,1,0:T(8,128)(2,1)}), bf16[4,16,64,256]{3,2,1,0:T(8,128)(2,1)}, u32[]{:S(2)}, u32[]{:S(2)}) async-start(bf16[4,16,64,256]{3,2,1,0:T(8,128)(2,1)} %bitcast.12), calls=%async_computation.2 | async-start | bytes 4194304 | tf_op jit(solution)/shard_map/all_to_all | solution.py:32
  36.4 138.4 %reduce-scatter.2.cloned.1.call-start = ((), (), s32[]{:S(2)}) async-start(), calls=%async_computation.4 | async-start | bytes 2129920 | tf_op jit(solution)/shard_map/reduce_scatter | solution.py:51
Sparse Core Ops, SparseCore 0:
  137.7 37.0 reduce-scatter.1
where the time goes:
time: 184 us; the launch traced here: 183 us
  waiting for transfers between devices  86.1 us (47%)
  blocking collectives  40.8 us (22%)
  starting transfers between devices  14.2 us (8%)
  between operations  13.5 us (7%)
  local copies, waits for them, and re-layouts  13.2 us (7%)
  matrix products  9.8 us (5%)
  other arithmetic  5.64 us (3%)
    all_to_all x1, waiting for transfers between devices, local(): lax.all_to_all(picked, 'row', split_axis=0, concat_axis=0, tiled=True)  43.5 us
    psum x1, blocking collectives, local(): pupil_rounded = lax.psum(partial_pupil, 'layer').astype(jnp.bfloat16)  40.8 us
    reduce_scatter x1, waiting for transfers between devices, local(): lax.psum_scatter(lax.dot_general(pupil_rounded, fitting, (((0,), (0,)), (...  37.2 us
    all_to_all x1, starting transfers between devices, local(): lax.all_to_all(send_weight, 'row', split_axis=0, concat_axis=0, tiled=True)  6.35 us
    dot_general x1, matrix products, local(): lax.dot_general(pupil_rounded, fitting, (((0,), (0,)), ((), ())), preferr...  6.23 us
    all_to_all x1, starting transfers between devices, local(): lax.all_to_all(picked, 'row', split_axis=0, concat_axis=0, tiled=True)  4.58 us
  transfers between devices with their start and end apart: 4, of which 4 were waited for; matrix products, arithmetic and copies ran while one was open for 5% of the time, Pallas kernels for 0%

commit v1 on v0

--- a/solution.py
+++ b/solution.py
@@ -1,10 +1,12 @@
 import jax
 import jax.numpy as jnp
 from jax import lax
+from jax.experimental import pallas as pl
+from jax.experimental.pallas import tpu as pltpu
 from jax.sharding import PartitionSpec as P
 
 
-def local(layers, table, fitting, owner, local_slice, block_index, weight_index):
+def local_rows(layers, table, fitting, owner, local_slice, block_index, weight_index):
     rows_dev = layers.shape[1]
     columns = layers.shape[2]
     slice_rows = table.shape[1]
@@ -58,6 +60,104 @@
     ).astype(jnp.bfloat16)
 
 
+def terms_kernel(own_ref, got_ref, table_ref, meta_ref, out_ref, total_ref):
+    entries = meta_ref.shape[2]
+    block_rows = table_ref.shape[2]
+    total_ref[...] = jnp.zeros_like(total_ref)
+    group = 8 if entries % 8 == 0 else 1
+    for part, rows_ref in enumerate((own_ref, got_ref)):
+
+        def step(index, carry):
+            terms = []
+            for offset in range(group):
+                entry = index * group + offset
+                start = pl.multiple_of(meta_ref[part, 1, entry] * block_rows, block_rows)
+                terms.append(
+                    jnp.dot(
+                        table_ref[meta_ref[part, 2, entry]],
+                        rows_ref[pl.ds(start, block_rows), :],
+                        preferred_element_type=jnp.float32,
+                    )
+                )
+            for offset in range(group):
+                place = meta_ref[part, 0, index * group + offset]
+                total_ref[place] += terms[offset]
+            return carry
+
+        lax.fori_loop(0, entries // group, step, 0)
+
+    def write(index, carry):
+        out_ref[index] = total_ref[index].astype(out_ref.dtype)
+        return carry
+
+    lax.fori_loop(0, out_ref.shape[0], write, 0)
+
+
+def local_reduced(layers, table, fitting, owner, local_slice, block_index, weight_index):
+    columns = layers.shape[2]
+    slice_rows = table.shape[1]
+    peer_count = lax.axis_size("row")
+    owned_slices = fitting.shape[0] // slice_rows
+    half_slices = owned_slices // 2
+    half_columns = columns // 2
+    slice_total = peer_count * owned_slices
+    me = lax.axis_index("layer")
+    core = me % 2
+    along = me // 2
+    swap_x = [(0, 2), (2, 0), (1, 3), (3, 1)]
+    swap_core = [(0, 1), (1, 0), (2, 3), (3, 2)]
+
+    local_now = local_slice[0]
+    place = (
+        (local_now // half_slices) * (peer_count * half_slices)
+        + owner[0, :, 0] * half_slices
+        + local_now % half_slices
+    )
+    meta = jnp.stack([place, block_index[0], weight_index[0]])
+    own = lax.dynamic_slice_in_dim(layers[0], along * half_columns, half_columns, 1)
+    other = lax.dynamic_slice_in_dim(layers[0], (1 - along) * half_columns, half_columns, 1)
+    got = lax.ppermute(other, "layer", swap_x)
+    got_meta = lax.ppermute(meta, "layer", swap_x)
+    partial = pl.pallas_call(
+        terms_kernel,
+        out_shape=jax.ShapeDtypeStruct((slice_total, slice_rows, half_columns), jnp.bfloat16),
+        in_specs=[pl.BlockSpec(memory_space=pltpu.VMEM)] * 3
+        + [pl.BlockSpec(memory_space=pltpu.SMEM)],
+        out_specs=pl.BlockSpec(memory_space=pltpu.VMEM),
+        scratch_shapes=[pltpu.VMEM((slice_total, slice_rows, half_columns), jnp.float32)],
+    )(own, got, table, jnp.stack([meta, got_meta]))
+    partial = partial.reshape(2, peer_count, half_slices * slice_rows, half_columns)
+    kept = lax.dynamic_index_in_dim(partial, core, 0, keepdims=False)
+    given = lax.dynamic_index_in_dim(partial, 1 - core, 0, keepdims=False)
+    both = (
+        kept.astype(jnp.float32) + lax.ppermute(given, "layer", swap_core).astype(jnp.float32)
+    ).astype(jnp.bfloat16)
+    arrived = lax.all_to_all(both, "row", split_axis=0, concat_axis=0, tiled=True)
+    piece = jnp.sum(arrived.astype(jnp.float32), axis=0).astype(jnp.bfloat16)
+    pieces = lax.all_gather(piece, "layer", axis=0, tiled=False)
+    pupil_rounded = (
+        pieces.reshape(2, 2, half_slices * slice_rows, half_columns)
+        .transpose(1, 2, 0, 3)
+        .reshape(owned_slices * slice_rows, columns)
+    )
+    product = lax.dot_general(
+        pupil_rounded, fitting, (((0,), (0,)), ((), ())), preferred_element_type=jnp.float32
+    ).astype(jnp.bfloat16)
+    product = product.reshape(peer_count, columns // peer_count, fitting.shape[1])
+    landed = lax.all_to_all(product, "row", split_axis=0, concat_axis=0, tiled=True)
+    return jnp.sum(landed.astype(jnp.float32), axis=0).astype(jnp.bfloat16)
+
+
+def local(layers, table, fitting, owner, local_slice, block_index, weight_index):
+    arguments = (layers, table, fitting, owner, local_slice, block_index, weight_index)
+    entries, peers, group = owner.shape[1], lax.axis_size("row"), lax.axis_size("layer")
+    raw_rows = max(2, 2 * entries // peers) * table.shape[2]
+    reduced_rows = fitting.shape[0] // group
+    if group == 4 and raw_rows > reduced_rows:
+        return local_reduced(*arguments)
+    return local_rows(*arguments)
+
+
 def solution(mesh):
     return jax.shard_map(
         local,

time: 184 us -> 126 us (0.68)
  waiting for transfers between devices: 86.1 us -> 29.5 us
  blocking collectives: 40.8 us -> 57.3 us
  starting transfers between devices: 14.2 us -> 3.15 us
  Pallas kernels: 0 us -> 5.3 us
  matrix products: 9.8 us -> 4.85 us
  local copies, waits for them, and re-layouts: 13.2 us -> 8.41 us
    all_to_all x0 -> x2, blocking collectives: none -> 57.3 us  [the longest x1 31 us: local_reduced(): lax.all_to_all(both, 'row', split_axis=0, concat_axis=0, tiled=True)]
    all_to_all x3 -> x0, waiting for transfers between devices: 48.9 us -> none  [the longest x1 43.5 us: local(): lax.all_to_all(picked, 'row', split_axis=0, concat_axis=0, tiled=True)]
    psum x1 -> x0, blocking collectives: 40.8 us -> none  [local(): pupil_rounded = lax.psum(partial_pupil, 'layer').astype(jnp.bfloat16)]
    reduce_scatter x1 -> x0, waiting for transfers between devices: 37.2 us -> none  [local(): lax.psum_scatter(lax.dot_general(pupil_rounded, fitting, (((0,), (0,)), (...]
    all_gather x0 -> x1, waiting for transfers between devices: none -> 16 us  [local_reduced(): pieces = lax.all_gather(piece, 'layer', axis=0, tiled=False)]
    all_to_all x3 -> x0, starting transfers between devices: 14.2 us -> none  [the longest x1 6.35 us: local(): lax.all_to_all(send_weight, 'row', split_axis=0, concat_axis=0, tiled=True)]
    ppermute x0 -> x3, waiting for transfers between devices: none -> 13.6 us  [the longest x1 10.8 us: local_reduced(): got_meta = lax.ppermute(meta, 'layer', swap_x)]
    gather x5 -> x0, local copies, waits for them, and re-layouts: 7.07 us -> none  [the longest x1 2.03 us: local(): grouped[block_index[0][source]]]
  transfers between devices with their start and end apart: 4 -> 4, of which waited for: 4 -> 3; matrix products, arithmetic and copies ran while one was open for 5% -> 1% of each run, Pallas kernels for 0% -> 0%
where the time goes in v1:
time: 126 us
  blocking collectives  57.3 us (45%)
  waiting for transfers between devices  29.5 us (23%)
  between operations  13.5 us (11%)
  local copies, waits for them, and re-layouts  8.41 us (7%)
  Pallas kernels  5.3 us (4%)
  matrix products  4.85 us (4%)
  other arithmetic  3.87 us (3%)
  starting transfers between devices  3.15 us (2%)
    all_to_all x1, blocking collectives, local_reduced(): lax.all_to_all(both, 'row', split_axis=0, concat_axis=0, tiled=True)  31 us
    all_to_all x1, blocking collectives, local_reduced(): lax.all_to_all(product, 'row', split_axis=0, concat_axis=0, tiled=True)  26.3 us
    all_gather x1, waiting for transfers between devices, local_reduced(): pieces = lax.all_gather(piece, 'layer', axis=0, tiled=False)  16 us
    ppermute x1, waiting for transfers between devices, local_reduced(): got_meta = lax.ppermute(meta, 'layer', swap_x)  10.8 us
    pallas_call x1, Pallas kernels, local_reduced(): pl.pallas_call(terms_kernel, out_shape=jax.ShapeDtypeStruct((slice_total,...  5.3 us
    dot_general x1, matrix products, local_reduced(): lax.dot_general(pupil_rounded, fitting, (((0,), (0,)), ((), ())), preferr...  4.85 us
    ppermute x1, starting transfers between devices, local_reduced(): got = lax.ppermute(other, 'layer', swap_x)  2.97 us
    ppermute x1, waiting for transfers between devices, local_reduced(): lax.ppermute(given, 'layer', swap_core).astype(jnp.float32)  2.77 us
  transfers between devices with their start and end apart: 4, of which 3 were waited for; matrix products, arithmetic and copies ran while one was open for 1% of the time, Pallas kernels for 0%

profile of v1, /device:TPU:0, one launch (start us, length us, event | category | flops | bytes accessed | tf_op | source)
XLA Modules:
  0.0 125.9 jit_solution(8613254293994291728)
XLA Ops:
  6.5 0.0 copy-start.6
  6.5 0.0 copy-start.5
  6.5 0.0 copy-start.3
  6.5 0.0 copy-start.4
  6.5 0.0 copy-start.2
  6.5 0.0 all-gather.3.cloned.1.call-start
  6.6 2.1 %dynamic-slice_bitcast_fusion.1 = (bf16[2048,128]{1,0:T(8,128)(2,1)S(1)}, bf16[2048,128]{1,0:T(8,128)(2,1)}) fusion(bf16[1,2048,256]{2,1,0:T(8,128)(2,1)} %param.7, s32[]{:T(128)S(6)} %select_n.39, s32[]{:T(128)S(6)} %select_n.38), kind=kLoop, calls=%fused_computation.6 | loop fusion | bytes 2097160 | tf_op jit(solution)/shard_map/dynamic_slice | solution.py:118
  8.8 3.0 %collective-permute-start = (bf16[2048,128]{1,0:T(8,128)(2,1)S(1)}, bf16[2048,128]{1,0:T(8,128)(2,1)S(1)}, u32[]{:S(2)}, u32[]{:S(2)}) collective-permute-start(bf16[2048,128]{1,0:T(8,128)(2,1)S(1)} %get-tuple-element.5), channel_id=1, source_target_pairs={{0,2},{2,0},{1,3},{3,1},{4,6},{6,4},{5,7},{7,5},{8,10},{10,8},{9,1... | collective-permute-start | bytes 1572872 | tf_op jit(solution)/shard_map/ppermute | solution.py:119
  11.7 0.0 copy-done.6
  11.7 0.0 copy-done.5
  11.7 0.0 copy-done.3
  11.7 0.0 copy-done.4
  11.8 0.1 collective-permute-start.1
  11.9 0.0 copy-done.2
  11.9 1.0 copy.11.table_ref
  12.9 10.8 %collective-permute-done.1 = s32[3,32]{1,0:T(4,128)S(1)} collective-permute-done((s32[3,32]{1,0:T(4,128)S(1)}, s32[3,32]{1,0:T(4,128)S(1)}, u32[]{:S(2)}, u32[]{:S(2)}) %collective-permute-start.1) | collective-permute-done | bytes 416 | tf_op jit(solution)/shard_map/ppermute | solution.py:120
  23.7 0.6 pad_add_fusion.meta_ref
  24.3 0.0 collective-permute-done.got_ref
  24.3 0.0 copy-start.1
  24.3 0.8 copy-done.1
  25.1 5.3 %shard_map.73 = bf16[64,128,128]{2,1,0:T(8,128)(2,1)} custom-call(bf16[2048,128]{1,0:T(8,128)(2,1)} %get-tuple-element.6.own_ref, bf16[2048,128]{1,0:T(8,128)(2,1)} %copy-done.1, bf16[16,128,64]{2,1,0:T(8,128)(2,1)} %copy.11.table_ref, s32[2,3,32]{2,1,0:T(4,128)} %pad_add_fusion.meta_ref), custom_call_target="tpu_custom_call" | custom-call | tf_op jit(solution)/shard_map/pallas_call | solution.py:121
  30.4 0.0 copy-start
  30.4 1.4 %dynamic-slice_bitcast_fusion = bf16[4,1024,128]{2,1,0:T(8,128)(2,1)S(1)} fusion(bf16[2,4,1024,128]{3,2,1,0:T(8,128)(2,1)} %bitcast.27, s32[]{:T(128)S(6)} %select_n.44), kind=kLoop, calls=%fused_computation.5 | loop fusion | bytes 2097156 | tf_op jit(solution)/shard_map/jit(dynamic_index_in_dim)/squeeze | solution.py:131
  31.8 0.1 collective-permute-start.2
  31.9 2.8 %collective-permute-done.2 = bf16[4,1024,128]{2,1,0:T(8,128)(2,1)} collective-permute-done((bf16[4,1024,128]{2,1,0:T(8,128)(2,1)S(1)}, bf16[4,1024,128]{2,1,0:T(8,128)(2,1)}, u32[]{:S(2)}, u32[]{:S(2)}) %collective-permute-start.2) | collective-permute-done | bytes 1048608 | tf_op jit(solution)/shard_map/ppermute | solution.py:133
  34.7 0.0 copy-done
  34.7 1.5 %fusion = bf16[4,1024,128]{2,1,0:T(8,128)(2,1)S(1)} fusion(bf16[4,1024,128]{2,1,0:T(8,128)(2,1)} %collective-permute-done.2, bf16[2,4,1024,128]{3,2,1,0:T(8,128)(2,1)S(1)} %bitcast.28, s32[]{:T(128)S(6)} %select_n.43), kind=kLoop, calls=%fused_computation.2 | loop fusion | flops 2097152 | bytes 3145732 | tf_op jit(solution)/shard_map/convert_element_type | solution.py:134
  36.2 31.0 %all_to_all.10 = bf16[4,1024,128]{2,1,0:T(8,128)(2,1)S(1)} all-to-all(bf16[4,1024,128]{2,1,0:T(8,128)(2,1)S(1)} %fusion), channel_id=1, replica_groups=mesh['panel'=2,'row'=4,'layer'=4] {'row'}, dimensions={0} | all-to-all | bytes 2097152 | tf_op jit(solution)/shard_map/all_to_all | solution.py:135
  67.2 0.9 reduce_sum.24
  68.1 0.0 all-gather.3.cloned.1.call-update
  68.1 16.0 %all-gather.3.cloned.1.call-done = bf16[4096,128]{1,0:T(8,128)(2,1)} async-done(((bf16[1024,128]{1,0:T(8,128)(2,1)}), bf16[4096,128]{1,0:T(8,128)(2,1)}) %all-gather.3.cloned.1.call-update) | async-done | bytes 1048592 | tf_op jit(solution)/shard_map/all_gather | solution.py:137
  84.0 2.3 %copy.12 = bf16[2,1024,2,128]{3,2,1,0:T(2,128)(2,1)S(1)} copy(bf16[2,1024,2,128]{3,1,0,2:T(8,128)(2,1)} %bitcast.30) | data formatting | bytes 2097152 | tf_op jit(solution)/shard_map/transpose | solution.py:140
  86.3 4.8 %convolution_convert_fusion = bf16[256,1650]{0,1:T(8,128)(2,1)S(1)} fusion(bf16[2048,1650]{0,1:T(8,128)(2,1)} %param.9, bf16[256,8,2,128]{3,2,1,0:T(2,128)(2,1)S(1)} %bitcast.31), kind=kOutput, calls=%fused_computation | convolution fusion | flops 1730572800 | bytes 8651776 | tf_op jit(solution)/shard_map/dot_general | solution.py:143
  91.2 0.7 copy.13
  91.9 26.3 %all_to_all.11 = bf16[4,64,1650]{2,1,0:T(8,128)(2,1)S(1)} all-to-all(bf16[4,64,1650]{2,1,0:T(8,128)(2,1)S(1)} %bitcast.29), channel_id=1, replica_groups=mesh['panel'=2,'row'=4,'layer'=4] {'row'}, dimensions={0} | all-to-all | bytes 1689600 | tf_op jit(solution)/shard_map/all_to_all | solution.py:147
  118.2 0.8 reduce_sum.25
  (2 shorter events, 0.0 us)
Async XLA Ops:
  6.5 5.2 %copy-start.6 = (s32[1,32]{1,0:T(1,128)S(1)}, s32[1,32]{1,0:T(1,128)}, u32[]{:S(2)}) copy-start(s32[1,32]{1,0:T(1,128)} %param.11) | copy-start | bytes 388
  6.5 5.2 %copy-start.5 = (s32[1,32,1]{1,2,0:T(1,128)S(1)}, s32[1,32,1]{1,2,0:T(1,128)}, u32[]{:S(2)}) copy-start(s32[1,32,1]{1,2,0:T(1,128)} %param.10) | copy-start | bytes 388
  6.5 5.2 %copy-start.3 = (s32[1,32]{1,0:T(1,128)S(1)}, s32[1,32]{1,0:T(1,128)}, u32[]{:S(2)}) copy-start(s32[1,32]{1,0:T(1,128)} %param.13) | copy-start | bytes 388
  6.5 5.2 %copy-start.4 = (s32[1,32]{1,0:T(1,128)S(1)}, s32[1,32]{1,0:T(1,128)}, u32[]{:S(2)}) copy-start(s32[1,32]{1,0:T(1,128)} %param.12) | copy-start | bytes 388
  6.5 5.3 %copy-start.2 = (bf16[16,128,64]{1,2,0:T(8,128)(2,1)S(1)}, bf16[16,128,64]{1,2,0:T(8,128)(2,1)}, u32[]{:S(2)}) copy-start(bf16[16,128,64]{1,2,0:T(8,128)(2,1)} %param.8) | copy-start | bytes 786436
  6.5 77.5 %all-gather.3.cloned.1.call-start = ((), (), s32[]{:S(2)}) async-start(), calls=%async_computation.2 | async-start | bytes 1310720 | tf_op jit(solution)/shard_map/all_gather | solution.py:137
  8.8 15.5 %collective-permute-start = (bf16[2048,128]{1,0:T(8,128)(2,1)S(1)}, bf16[2048,128]{1,0:T(8,128)(2,1)S(1)}, u32[]{:S(2)}, u32[]{:S(2)}) collective-permute-start(bf16[2048,128]{1,0:T(8,128)(2,1)S(1)} %get-tuple-element.5), channel_id=1, source_target_pairs={{0,2},{2,0},{1,3},{3,1},{4,6},{6,4},{5,7},{7,5},{8,10},{10,8},{9,1... | collective-permute-start | bytes 1572872 | tf_op jit(solution)/shard_map/ppermute | solution.py:119
  11.8 11.9 %collective-permute-start.1 = (s32[3,32]{1,0:T(4,128)S(1)}, s32[3,32]{1,0:T(4,128)S(1)}, u32[]{:S(2)}, u32[]{:S(2)}) collective-permute-start(s32[3,32]{1,0:T(4,128)S(1)} %get-tuple-element.8), channel_id=1, source_target_pairs={{0,2},{2,0},{1,3},{3,1},{4,6},{6,4},{5,7},{7,5},{8,10},{10,8},{9,1... | collective-permute-start | bytes 1160 | tf_op jit(solution)/shard_map/ppermute | solution.py:120
  24.3 0.8 copy-start.1
  30.4 4.3 %copy-start = (bf16[64,128,128]{2,1,0:T(8,128)(2,1)S(1)}, bf16[64,128,128]{2,1,0:T(8,128)(2,1)}, u32[]{:S(2)}) copy-start(bf16[64,128,128]{2,1,0:T(8,128)(2,1)} %shard_map.73) | copy-start | bytes 6291460
  31.8 2.9 %collective-permute-start.2 = (bf16[4,1024,128]{2,1,0:T(8,128)(2,1)S(1)}, bf16[4,1024,128]{2,1,0:T(8,128)(2,1)}, u32[]{:S(2)}, u32[]{:S(2)}) collective-permute-start(bf16[4,1024,128]{2,1,0:T(8,128)(2,1)S(1)} %dynamic-slice_bitcast_fusion), channel_id=1, source_target_pairs={{0,1},{1,0},{2,3},{3,2},{4,5},{5,4},{6,7},{7,6},{8,9},{9,8},{10,11... | collective-permute-start | bytes 3145736 | tf_op jit(solution)/shard_map/ppermute | solution.py:133
Sparse Core Ops, SparseCore 0:
  68.2 15.7 all-gather.2

commit v2 on v1

--- a/solution.py
+++ b/solution.py
@@ -1,8 +1,12 @@
+import functools
+
 import jax
 import jax.numpy as jnp
 from jax import lax
 from jax.experimental import pallas as pl
 from jax.experimental.pallas import tpu as pltpu
+
+MESH = pl.DeviceIdType.MESH
 from jax.sharding import PartitionSpec as P
 
 
@@ -93,6 +97,197 @@
     lax.fori_loop(0, out_ref.shape[0], write, 0)
 
 
+def exchange_kernel(
+    peers, part_ref, fitting_ref, out_ref,
+    fit, core_in, both, row_in, pieces, total, product, landed,
+    fit_sem, core_send, core_recv, row_send, row_recv, layer_send, layer_recv, end_send, end_recv,
+):
+    row = lax.axis_index("row")
+    me = lax.axis_index("layer")
+    core = lax.rem(me, 2)
+    steps = core_send.shape[0]
+    piece_rows = pieces.shape[1]
+    rows = piece_rows // steps
+    width = fit.shape[1]
+    half_columns = pieces.shape[2]
+    out_rows = out_ref.shape[0]
+    row_peers = [lax.rem(row + k, peers) for k in range(1, peers)]
+    layer_peers = [lax.rem(me + k, 4) for k in range(1, 4)]
+
+    fit_copy = pltpu.make_async_copy(fitting_ref, fit, fit_sem)
+    fit_copy.start()
+    barrier = pltpu.get_barrier_semaphore()
+    for peer in row_peers:
+        pl.semaphore_signal(barrier, inc=1, device_id={"row": peer}, device_id_type=MESH)
+    for peer in layer_peers:
+        pl.semaphore_signal(barrier, inc=1, device_id={"layer": peer}, device_id_type=MESH)
+    pl.semaphore_wait(barrier, peers - 1 + 3)
+
+    core_copies = []
+    for step in range(steps):
+        copy = pltpu.make_async_remote_copy(
+            src_ref=part_ref.at[1 - core, :, pl.ds(step * rows, rows), :],
+            dst_ref=core_in.at[:, pl.ds(step * rows, rows), :],
+            send_sem=core_send.at[step],
+            recv_sem=core_recv.at[step],
+            device_id={"layer": me + 1 - 2 * core},
+            device_id_type=MESH,
+        )
+        copy.start()
+        core_copies.append(copy)
+
+    row_copies = []
+    for step in range(steps):
+        part = slice(step * rows, (step + 1) * rows)
+        core_copies[step].wait_recv()
+        both[:, part, :] = (
+            part_ref[core, :, part, :].astype(jnp.float32) + core_in[:, part, :].astype(jnp.float32)
+        ).astype(both.dtype)
+        sent = []
+        for k, peer in enumerate(row_peers):
+            copy = pltpu.make_async_remote_copy(
+                src_ref=both.at[peer, pl.ds(step * rows, rows), :],
+                dst_ref=row_in.at[k, pl.ds(step * rows, rows), :],
+                send_sem=row_send.at[k, step],
+                recv_sem=row_recv.at[k, step],
+                device_id={"row": peer},
+                device_id_type=MESH,
+            )
+            copy.start()
+            sent.append(copy)
+        row_copies.append(sent)
+
+    tiles = [(start, min(start + 512, width)) for start in range(0, width, 512)]
+
+    def multiply(step):
+        for start, stop in tiles:
+            value = None
+            for half in range(2):
+                part = slice(step * rows, (step + 1) * rows)
+                left = jnp.concatenate([pieces[half, part, :], pieces[2 + half, part, :]], axis=1)
+                first = half * piece_rows + step * rows
+                term = lax.dot_general(
+                    left,
+                    fit[first : first + rows, start:stop],
+                    (((0,), (0,)), ((), ())),
+                    preferred_element_type=jnp.float32,
+                )
+                value = term if value is None else value + term
+            if step == 0:
+                total[:, start:stop] = value
+            else:
+                total[:, start:stop] += value
+
+    layer_copies = []
+    for step in range(steps):
+        part = slice(step * rows, (step + 1) * rows)
+        for copy in row_copies[step]:
+            copy.wait_recv()
+        value = both[row, part, :].astype(jnp.float32)
+        for k in range(peers - 1):
+            value = value + row_in[k, part, :].astype(jnp.float32)
+        pieces[me, part, :] = value.astype(pieces.dtype)
+        sent = []
+        for k, peer in enumerate(layer_peers):
+            copy = pltpu.make_async_remote_copy(
+                src_ref=pieces.at[me, pl.ds(step * rows, rows), :],
+                dst_ref=pieces.at[me, pl.ds(step * rows, rows), :],
+                send_sem=layer_send.at[k, step],
+                recv_sem=layer_recv.at[k, step],
+                device_id={"layer": peer},
+                device_id_type=MESH,
+            )
+            copy.start()
+            sent.append(copy)
+        layer_copies.append(sent)
+        if step == 0:
+            fit_copy.wait()
+        if step > 0:
+            for copy in layer_copies[step - 1]:
+                copy.wait_recv()
+            multiply(step - 1)
+    for copy in layer_copies[steps - 1]:
+        copy.wait_recv()
+    multiply(steps - 1)
+
+    padded = product.shape[2]
+    cuts = [0, padded // 256 * 128, padded]
+    if width < padded:
+        product[:, :, padded - 128 :] = jnp.zeros((peers, out_rows, 128), product.dtype)
+    end_copies = []
+    for cut in range(2):
+        lanes = slice(cuts[cut], min(cuts[cut + 1], width))
+        for peer in range(peers):
+            product[peer, :, lanes] = total[
+                peer * out_rows : (peer + 1) * out_rows, lanes
+            ].astype(product.dtype)
+        sent = []
+        for k, peer in enumerate(row_peers):
+            span = pl.ds(cuts[cut], cuts[cut + 1] - cuts[cut])
+            copy = pltpu.make_async_remote_copy(
+                src_ref=product.at[peer, :, span],
+                dst_ref=landed.at[k, :, span],
+                send_sem=end_send.at[k, cut],
+                recv_sem=end_recv.at[k, cut],
+                device_id={"row": peer},
+                device_id_type=MESH,
+            )
+            copy.start()
+            sent.append(copy)
+        end_copies.append(sent)
+    for cut in range(2):
+        lanes = slice(cuts[cut], min(cuts[cut + 1], width))
+        for copy in end_copies[cut]:
+            copy.wait_recv()
+        value = total[pl.ds(pl.multiple_of(row * out_rows, out_rows), out_rows), lanes]
+        for k in range(peers - 1):
+            value = value + landed[k, :, lanes].astype(jnp.float32)
+        out_ref[:, lanes] = value.astype(out_ref.dtype)
+
+    for copy in core_copies:
+        copy.wait_send()
+    for copies in (row_copies, layer_copies, end_copies):
+        for sent in copies:
+            for copy in sent:
+                copy.wait_send()
+
+
+def exchange(partial, fitting):
+    _, peers, piece_rows, half_columns = partial.shape
+    depth, width = fitting.shape
+    columns = 2 * half_columns
+    out_rows = columns // peers
+    padded = -(-width // 128) * 128
+    steps = 4
+    dma = pltpu.SemaphoreType.DMA
+    return pl.pallas_call(
+        functools.partial(exchange_kernel, peers),
+        out_shape=jax.ShapeDtypeStruct((out_rows, width), jnp.bfloat16),
+        in_specs=[pl.BlockSpec(memory_space=pltpu.VMEM), pl.BlockSpec(memory_space=pl.ANY)],
+        out_specs=pl.BlockSpec(memory_space=pltpu.VMEM),
+        scratch_shapes=[
+            pltpu.VMEM((depth, width), jnp.bfloat16),
+            pltpu.VMEM((peers, piece_rows, half_columns), jnp.bfloat16),
+            pltpu.VMEM((peers, piece_rows, half_columns), jnp.bfloat16),
+            pltpu.VMEM((peers - 1, piece_rows, half_columns), jnp.bfloat16),
+            pltpu.VMEM((4, piece_rows, half_columns), jnp.bfloat16),
+            pltpu.VMEM((columns, width), jnp.float32),
+            pltpu.VMEM((peers, out_rows, padded), jnp.bfloat16),
+            pltpu.VMEM((peers - 1, out_rows, padded), jnp.bfloat16),
+            dma,
+            dma((steps,)),
+            dma((steps,)),
+            dma((peers - 1, steps)),
+            dma((peers - 1, steps)),
+            dma((3, steps)),
+            dma((3, steps)),
+            dma((peers - 1, 2)),
+            dma((peers - 1, 2)),
+        ],
+        compiler_params=pltpu.CompilerParams(collective_id=0, has_side_effects=True),
+    )(partial, fitting)
+
+
 def local_reduced(layers, table, fitting, owner, local_slice, block_index, weight_index):
     columns = layers.shape[2]
     slice_rows = table.shape[1]
@@ -102,10 +297,8 @@
     half_columns = columns // 2
     slice_total = peer_count * owned_slices
     me = lax.axis_index("layer")
-    core = me % 2
     along = me // 2
     swap_x = [(0, 2), (2, 0), (1, 3), (3, 1)]
-    swap_core = [(0, 1), (1, 0), (2, 3), (3, 2)]
 
     local_now = local_slice[0]
     place = (
@@ -127,25 +320,7 @@
         scratch_shapes=[pltpu.VMEM((slice_total, slice_rows, half_columns), jnp.float32)],
     )(own, got, table, jnp.stack([meta, got_meta]))
     partial = partial.reshape(2, peer_count, half_slices * slice_rows, half_columns)
-    kept = lax.dynamic_index_in_dim(partial, core, 0, keepdims=False)
-    given = lax.dynamic_index_in_dim(partial, 1 - core, 0, keepdims=False)
-    both = (
-        kept.astype(jnp.float32) + lax.ppermute(given, "layer", swap_core).astype(jnp.float32)
-    ).astype(jnp.bfloat16)
-    arrived = lax.all_to_all(both, "row", split_axis=0, concat_axis=0, tiled=True)
-    piece = jnp.sum(arrived.astype(jnp.float32), axis=0).astype(jnp.bfloat16)
-    pieces = lax.all_gather(piece, "layer", axis=0, tiled=False)
-    pupil_rounded = (
-        pieces.reshape(2, 2, half_slices * slice_rows, half_columns)
-        .transpose(1, 2, 0, 3)
-        .reshape(owned_slices * slice_rows, columns)
-    )
-    product = lax.dot_general(
-        pupil_rounded, fitting, (((0,), (0,)), ((), ())), preferred_element_type=jnp.float32
-    ).astype(jnp.bfloat16)
-    product = product.reshape(peer_count, columns // peer_count, fitting.shape[1])
-    landed = lax.all_to_all(product, "row", split_axis=0, concat_axis=0, tiled=True)
-    return jnp.sum(landed.astype(jnp.float32), axis=0).astype(jnp.bfloat16)
+    return exchange(partial, fitting)
 
 
 def local(layers, table, fitting, owner, local_slice, block_index, weight_index):

time: 126 us -> 81.4 us (0.65)
  blocking collectives: 57.3 us -> 0 us
  Pallas kernels: 5.3 us -> 59.6 us
  waiting for transfers between devices: 29.5 us -> 0.01 us
  between operations: 13.5 us -> 0.02 us
  local copies, waits for them, and re-layouts: 8.41 us -> 16.2 us
  matrix products: 4.85 us -> 0 us
  other arithmetic: 3.87 us -> 1.96 us
    all_to_all x2 -> x0, blocking collectives: 57.3 us -> none  [the longest x1 31 us: local_reduced(): lax.all_to_all(both, 'row', split_axis=0, concat_axis=0, tiled=True)]
    pallas_call x0 -> x1, Pallas kernels: none -> 54.2 us  [exchange(): pl.pallas_call(functools.partial(exchange_kernel, peers), out_shape=jax.S...]
    all_gather x1 -> x0, waiting for transfers between devices: 16 us -> none  [local_reduced(): pieces = lax.all_gather(piece, 'layer', axis=0, tiled=False)]
    unnamed x15 -> x5, local copies, waits for them, and re-layouts: 1.84 us -> 14.1 us
    ppermute x1, waiting for transfers between devices: 10.8 us -> 0.01 us  [local_reduced(): got_meta = lax.ppermute(meta, 'layer', swap_x)]
    dot_general x1 -> x0, matrix products: 4.85 us -> none  [local_reduced(): lax.dot_general(pupil_rounded, fitting, (((0,), (0,)), ((), ())), preferr...]
    ppermute x1 -> x0, waiting for transfers between devices: 2.77 us -> none  [local_reduced(): lax.ppermute(given, 'layer', swap_core).astype(jnp.float32)]
    transpose x1 -> x0, local copies, waits for them, and re-layouts: 2.3 us -> none  [local_reduced(): pupil_rounded = pieces.reshape(2, 2, half_slices * slice_rows, half_colum...]
  transfers between devices with their start and end apart: 4 -> 2, of which waited for: 3 -> 0; matrix products, arithmetic and copies ran while one was open for 1% -> 17% of each run, Pallas kernels for 0% -> 0%
where the time goes in v2:
time: 81.4 us; the launch traced here: 80.8 us
  Pallas kernels  59.6 us (73%)
  local copies, waits for them, and re-layouts  16.2 us (20%)
  starting transfers between devices  3.02 us (4%)
  other arithmetic  1.96 us (2%)
    pallas_call x1, Pallas kernels, exchange(): pl.pallas_call(functools.partial(exchange_kernel, peers), out_shape=jax.S...  54.2 us
    unnamed x5, local copies, waits for them, and re-layouts  14.1 us
    pallas_call x1, Pallas kernels, local_reduced(): pl.pallas_call(terms_kernel, out_shape=jax.ShapeDtypeStruct((slice_total,...  5.36 us
    ppermute x1, starting transfers between devices, local_reduced(): got = lax.ppermute(other, 'layer', swap_x)  2.97 us
    dynamic_slice x1, local copies, waits for them, and re-layouts, local_reduced(): lax.dynamic_slice_in_dim(layers[0], (1 - along) * half_columns, half_colu...  2.1 us
  transfers between devices with their start and end apart: 2, of which 0 were waited for; matrix products, arithmetic and copies ran while one was open for 17% of the time, Pallas kernels for 0%

profile of v2, /device:TPU:0, one launch (start us, length us, event | category | flops | bytes accessed | tf_op | source)
XLA Modules:
  0.0 80.8 jit_solution(13681762769283651865)
XLA Ops:
  0.0 2.1 %dynamic-slice_bitcast_fusion = (bf16[2048,128]{1,0:T(8,128)(2,1)S(1)}, bf16[2048,128]{1,0:T(8,128)(2,1)}) fusion(bf16[1,2048,256]{2,1,0:T(8,128)(2,1)} %param.7, s32[]{:T(128)S(6)} %select_n.26, s32[]{:T(128)S(6)} %select_n.25), kind=kLoop, calls=%fused_computation | loop fusion | bytes 2097160 | tf_op jit(solution)/shard_map/dynamic_slice | solution.py:311
  2.1 3.0 %collective-permute-start = (bf16[2048,128]{1,0:T(8,128)(2,1)S(1)}, bf16[2048,128]{1,0:T(8,128)(2,1)S(1)}, u32[]{:S(2)}, u32[]{:S(2)}) collective-permute-start(bf16[2048,128]{1,0:T(8,128)(2,1)S(1)} %get-tuple-element.5), channel_id=1, source_target_pairs={{0,2},{2,0},{1,3},{3,1},{4,6},{6,4},{5,7},{7,5},{8,10},{10,8},{9,1... | collective-permute-start | bytes 1572872 | tf_op jit(solution)/shard_map/ppermute | solution.py:312
  5.1 0.7 fusion
  5.8 0.7 fusion.1
  6.4 0.1 collective-permute-start.1
  6.5 1.9 %copy.8.table_ref = bf16[16,128,64]{2,1,0:T(8,128)(2,1)} copy(bf16[16,128,64]{1,2,0:T(8,128)(2,1)} %param.8) | data formatting | bytes 524288 | tf_op args[1]
  8.4 9.8 %copy.9.fitting_ref = bf16[2048,1650]{1,0:T(8,128)(2,1)} copy(bf16[2048,1650]{0,1:T(8,128)(2,1)} %param.9) | data formatting | bytes 13516800 | tf_op args[2]
  18.2 0.0 collective-permute-done.1
  18.2 0.6 pad_add_fusion.meta_ref
  18.8 0.0 collective-permute-done.got_ref
  18.8 0.0 copy-start
  18.8 0.8 copy-done
  19.6 5.4 %shard_map.73 = bf16[64,128,128]{2,1,0:T(8,128)(2,1)} custom-call(bf16[2048,128]{1,0:T(8,128)(2,1)} %get-tuple-element.6.own_ref, bf16[2048,128]{1,0:T(8,128)(2,1)} %copy-done, bf16[16,128,64]{2,1,0:T(8,128)(2,1)} %copy.8.table_ref, s32[2,3,32]{2,1,0:T(4,128)} %pad_add_fusion.meta_ref), custom_call_target="tpu_custom_call" | custom-call | tf_op jit(solution)/shard_map/pallas_call | solution.py:314
  25.0 54.2 %shard_map.74 = bf16[64,1650]{1,0:T(8,128)(2,1)} custom-call(bf16[2,4,1024,128]{3,2,1,0:T(8,128)(2,1)} %bitcast.12, bf16[2048,1650]{1,0:T(8,128)(2,1)} %copy.9.fitting_ref), custom_call_target="tpu_custom_call" | custom-call | tf_op jit(solution)/shard_map/pallas_call | solution.py:263
  79.2 1.6 %copy.11 = bf16[64,1650]{1,0:T(8,128)(2,1)} copy(bf16[64,1650]{1,0:T(8,128)(2,1)} %shard_map.74) | data formatting | bytes 422400
Async XLA Ops:
  2.1 16.7 %collective-permute-start = (bf16[2048,128]{1,0:T(8,128)(2,1)S(1)}, bf16[2048,128]{1,0:T(8,128)(2,1)S(1)}, u32[]{:S(2)}, u32[]{:S(2)}) collective-permute-start(bf16[2048,128]{1,0:T(8,128)(2,1)S(1)} %get-tuple-element.5), channel_id=1, source_target_pairs={{0,2},{2,0},{1,3},{3,1},{4,6},{6,4},{5,7},{7,5},{8,10},{10,8},{9,1... | collective-permute-start | bytes 1572872 | tf_op jit(solution)/shard_map/ppermute | solution.py:312
  6.4 11.8 %collective-permute-start.1 = (s32[3,32]{1,0:T(4,128)S(1)}, s32[3,32]{1,0:T(4,128)S(1)}, u32[]{:S(2)}, u32[]{:S(2)}) collective-permute-start(s32[3,32]{1,0:T(4,128)S(1)} %get-tuple-element.8), channel_id=1, source_target_pairs={{0,2},{2,0},{1,3},{3,1},{4,6},{6,4},{5,7},{7,5},{8,10},{10,8},{9,1... | collective-permute-start | bytes 1160 | tf_op jit(solution)/shard_map/ppermute | solution.py:313
  18.8 0.8 copy-start

commit v3 on v2

--- a/solution.py
+++ b/solution.py
@@ -111,13 +111,17 @@
     width = fit.shape[1]
     half_columns = pieces.shape[2]
     out_rows = out_ref.shape[0]
-    row_peers = [lax.rem(row + k, peers) for k in range(1, peers)]
+    mate = row + 1 - 2 * lax.rem(row, 2)
+    cross = lax.rem(row + 2, peers)
+    opposite = peers - 1 - row
+    is_end = jnp.logical_or(row == 0, row == peers - 1)
+    is_middle = jnp.logical_not(is_end)
     layer_peers = [lax.rem(me + k, 4) for k in range(1, 4)]
 
     fit_copy = pltpu.make_async_copy(fitting_ref, fit, fit_sem)
     fit_copy.start()
     barrier = pltpu.get_barrier_semaphore()
-    for peer in row_peers:
+    for peer in (mate, cross, opposite):
         pl.semaphore_signal(barrier, inc=1, device_id={"row": peer}, device_id_type=MESH)
     for peer in layer_peers:
         pl.semaphore_signal(barrier, inc=1, device_id={"layer": peer}, device_id_type=MESH)
@@ -136,26 +140,45 @@
         copy.start()
         core_copies.append(copy)
 
-    row_copies = []
+    def row_copy(slot, step, source, peer):
+        part = pl.ds(step * rows, rows)
+        return pltpu.make_async_remote_copy(
+            src_ref=both.at[source, part, :],
+            dst_ref=row_in.at[slot, part, :],
+            send_sem=row_send.at[slot, step],
+            recv_sem=row_recv.at[slot, step],
+            device_id={"row": peer},
+            device_id_type=MESH,
+        )
+
     for step in range(steps):
         part = slice(step * rows, (step + 1) * rows)
         core_copies[step].wait_recv()
         both[:, part, :] = (
             part_ref[core, :, part, :].astype(jnp.float32) + core_in[:, part, :].astype(jnp.float32)
         ).astype(both.dtype)
-        sent = []
-        for k, peer in enumerate(row_peers):
-            copy = pltpu.make_async_remote_copy(
-                src_ref=both.at[peer, pl.ds(step * rows, rows), :],
-                dst_ref=row_in.at[k, pl.ds(step * rows, rows), :],
-                send_sem=row_send.at[k, step],
-                recv_sem=row_recv.at[k, step],
-                device_id={"row": peer},
-                device_id_type=MESH,
-            )
-            copy.start()
-            sent.append(copy)
-        row_copies.append(sent)
+
+        @pl.when(is_end)
+        def _():
+            row_copy(3, step, opposite, mate).start()
+            row_copy(1, step, cross, cross).start()
+
+        @pl.when(is_middle)
+        def _():
+            row_copy(2, step, opposite, opposite).start()
+
+        row_copy(0, step, mate, mate).start()
+
+    def join(step):
+        part = slice(step * rows, (step + 1) * rows)
+
+        @pl.when(is_middle)
+        def _():
+            row_copy(3, step, opposite, mate).wait_recv()
+            both[cross, part, :] = (
+                both[cross, part, :].astype(jnp.float32) + row_in[3, part, :].astype(jnp.float32)
+            ).astype(both.dtype)
+            row_copy(1, step, cross, cross).start()
 
     tiles = [(start, min(start + 512, width)) for start in range(0, width, 512)]
 
@@ -179,14 +202,27 @@
                 total[:, start:stop] += value
 
     layer_copies = []
+    join(0)
     for step in range(steps):
         part = slice(step * rows, (step + 1) * rows)
-        for copy in row_copies[step]:
-            copy.wait_recv()
-        value = both[row, part, :].astype(jnp.float32)
-        for k in range(peers - 1):
-            value = value + row_in[k, part, :].astype(jnp.float32)
-        pieces[me, part, :] = value.astype(pieces.dtype)
+        row_copy(0, step, mate, mate).wait_recv()
+        row_copy(1, step, cross, cross).wait_recv()
+
+        @pl.when(is_end)
+        def _():
+            value = both[row, part, :].astype(jnp.float32)
+            for slot in range(2):
+                value = value + row_in[slot, part, :].astype(jnp.float32)
+            pieces[me, part, :] = value.astype(pieces.dtype)
+
+        @pl.when(is_middle)
+        def _():
+            row_copy(2, step, opposite, opposite).wait_recv()
+            value = both[row, part, :].astype(jnp.float32)
+            for slot in range(3):
+                value = value + row_in[slot, part, :].astype(jnp.float32)
+            pieces[me, part, :] = value.astype(pieces.dtype)
+
         sent = []
         for k, peer in enumerate(layer_peers):
             copy = pltpu.make_async_remote_copy(
@@ -200,6 +236,8 @@
             copy.start()
             sent.append(copy)
         layer_copies.append(sent)
+        if step + 1 < steps:
+            join(step + 1)
         if step == 0:
             fit_copy.wait()
         if step > 0:
@@ -211,45 +249,97 @@
     multiply(steps - 1)
 
     padded = product.shape[2]
-    cuts = [0, padded // 256 * 128, padded]
+    pieces_out = end_send.shape[1]
+    cuts = [padded // 128 * cut // pieces_out * 128 for cut in range(pieces_out + 1)]
     if width < padded:
         product[:, :, padded - 128 :] = jnp.zeros((peers, out_rows, 128), product.dtype)
-    end_copies = []
-    for cut in range(2):
-        lanes = slice(cuts[cut], min(cuts[cut + 1], width))
-        for peer in range(peers):
-            product[peer, :, lanes] = total[
-                peer * out_rows : (peer + 1) * out_rows, lanes
-            ].astype(product.dtype)
-        sent = []
-        for k, peer in enumerate(row_peers):
-            span = pl.ds(cuts[cut], cuts[cut + 1] - cuts[cut])
-            copy = pltpu.make_async_remote_copy(
-                src_ref=product.at[peer, :, span],
-                dst_ref=landed.at[k, :, span],
-                send_sem=end_send.at[k, cut],
-                recv_sem=end_recv.at[k, cut],
-                device_id={"row": peer},
-                device_id_type=MESH,
-            )
-            copy.start()
-            sent.append(copy)
-        end_copies.append(sent)
-    for cut in range(2):
-        lanes = slice(cuts[cut], min(cuts[cut + 1], width))
-        for copy in end_copies[cut]:
-            copy.wait_recv()
-        value = total[pl.ds(pl.multiple_of(row * out_rows, out_rows), out_rows), lanes]
-        for k in range(peers - 1):
-            value = value + landed[k, :, lanes].astype(jnp.float32)
-        out_ref[:, lanes] = value.astype(out_ref.dtype)
+
+    def end_copy(slot, cut, source, peer):
+        span = pl.ds(cuts[cut], cuts[cut + 1] - cuts[cut])
+        return pltpu.make_async_remote_copy(
+            src_ref=product.at[source, :, span],
+            dst_ref=landed.at[slot, :, span],
+            send_sem=end_send.at[slot, cut],
+            recv_sem=end_recv.at[slot, cut],
+            device_id={"row": peer},
+            device_id_type=MESH,
+        )
+
+    def lanes_of(cut):
+        return slice(cuts[cut], min(cuts[cut + 1], width))
+
+    def total_of(owner, lanes):
+        return total[pl.ds(pl.multiple_of(owner * out_rows, out_rows), out_rows), lanes]
+
+    for cut in range(pieces_out):
+        lanes = lanes_of(cut)
+
+        @pl.when(is_end)
+        def _():
+            for peer in (opposite, cross, mate):
+                product[peer, :, lanes] = total_of(peer, lanes).astype(product.dtype)
+            end_copy(3, cut, opposite, mate).start()
+            end_copy(1, cut, cross, cross).start()
+            end_copy(0, cut, mate, mate).start()
+
+        @pl.when(is_middle)
+        def _():
+            for peer in (opposite, mate):
+                product[peer, :, lanes] = total_of(peer, lanes).astype(product.dtype)
+            end_copy(2, cut, opposite, opposite).start()
+            end_copy(0, cut, mate, mate).start()
+
+    @pl.when(is_middle)
+    def _():
+        for cut in range(pieces_out):
+            lanes = lanes_of(cut)
+            end_copy(3, cut, opposite, mate).wait_recv()
+            product[cross, :, lanes] = (
+                total_of(cross, lanes) + landed[3, :, lanes].astype(jnp.float32)
+            ).astype(product.dtype)
+            end_copy(1, cut, cross, cross).start()
+
+    for cut in range(pieces_out):
+        lanes = lanes_of(cut)
+        end_copy(0, cut, mate, mate).wait_recv()
+        end_copy(1, cut, cross, cross).wait_recv()
+
+        @pl.when(is_end)
+        def _():
+            value = total_of(row, lanes)
+            for slot in range(2):
+                value = value + landed[slot, :, lanes].astype(jnp.float32)
+            out_ref[:, lanes] = value.astype(out_ref.dtype)
+
+        @pl.when(is_middle)
+        def _():
+            end_copy(2, cut, opposite, opposite).wait_recv()
+            value = total_of(row, lanes)
+            for slot in range(3):
+                value = value + landed[slot, :, lanes].astype(jnp.float32)
+            out_ref[:, lanes] = value.astype(out_ref.dtype)
 
     for copy in core_copies:
         copy.wait_send()
-    for copies in (row_copies, layer_copies, end_copies):
-        for sent in copies:
-            for copy in sent:
-                copy.wait_send()
+    for sent in layer_copies:
+        for copy in sent:
+            copy.wait_send()
+
+    def finish(copy_of, count):
+        for index in range(count):
+            copy_of(0, index, mate, mate).wait_send()
+            copy_of(1, index, cross, cross).wait_send()
+
+            @pl.when(is_end)
+            def _():
+                copy_of(3, index, opposite, mate).wait_send()
+
+            @pl.when(is_middle)
+            def _():
+                copy_of(2, index, opposite, opposite).wait_send()
+
+    finish(row_copy, steps)
+    finish(end_copy, pieces_out)
 
 
 def exchange(partial, fitting):
@@ -269,20 +359,20 @@
             pltpu.VMEM((depth, width), jnp.bfloat16),
             pltpu.VMEM((peers, piece_rows, half_columns), jnp.bfloat16),
             pltpu.VMEM((peers, piece_rows, half_columns), jnp.bfloat16),
-            pltpu.VMEM((peers - 1, piece_rows, half_columns), jnp.bfloat16),
+            pltpu.VMEM((4, piece_rows, half_columns), jnp.bfloat16),
             pltpu.VMEM((4, piece_rows, half_columns), jnp.bfloat16),
             pltpu.VMEM((columns, width), jnp.float32),
             pltpu.VMEM((peers, out_rows, padded), jnp.bfloat16),
-            pltpu.VMEM((peers - 1, out_rows, padded), jnp.bfloat16),
+            pltpu.VMEM((4, out_rows, padded), jnp.bfloat16),
             dma,
             dma((steps,)),
             dma((steps,)),
-            dma((peers - 1, steps)),
-            dma((peers - 1, steps)),
+            dma((4, steps)),
+            dma((4, steps)),
             dma((3, steps)),
             dma((3, steps)),
-            dma((peers - 1, 2)),
-            dma((peers - 1, 2)),
+            dma((4, 3)),
+            dma((4, 3)),
         ],
         compiler_params=pltpu.CompilerParams(collective_id=0, has_side_effects=True),
     )(partial, fitting)
@@ -328,7 +418,7 @@
     entries, peers, group = owner.shape[1], lax.axis_size("row"), lax.axis_size("layer")
     raw_rows = max(2, 2 * entries // peers) * table.shape[2]
     reduced_rows = fitting.shape[0] // group
-    if group == 4 and raw_rows > reduced_rows:
+    if group == 4 and peers == 4 and raw_rows > reduced_rows:
         return local_reduced(*arguments)
     return local_rows(*arguments)
 

time: 81.4 us -> 76.8 us (0.943)
  Pallas kernels: 59.6 us -> 55.1 us
    pallas_call x1, Pallas kernels: 54.2 us -> 49.7 us  [exchange(): pl.pallas_call(functools.partial(exchange_kernel, peers), out_shape=jax.S...]
  transfers between devices with their start and end apart: 2 -> 2, of which waited for: 0 -> 0; matrix products, arithmetic and copies ran while one was open for 17% -> 18% of each run, Pallas kernels for 0% -> 0%
where the time goes in v3:
time: 76.8 us; the launch traced here: 76.3 us
  Pallas kernels  55.1 us (72%)
  local copies, waits for them, and re-layouts  16.2 us (21%)
  starting transfers between devices  3.02 us (4%)
  other arithmetic  1.96 us (3%)
    pallas_call x1, Pallas kernels, exchange(): pl.pallas_call(functools.partial(exchange_kernel, peers), out_shape=jax.S...  49.7 us
    unnamed x5, local copies, waits for them, and re-layouts  14.1 us
    pallas_call x1, Pallas kernels, local_reduced(): pl.pallas_call(terms_kernel, out_shape=jax.ShapeDtypeStruct((slice_total,...  5.36 us
    ppermute x1, starting transfers between devices, local_reduced(): got = lax.ppermute(other, 'layer', swap_x)  2.97 us
    dynamic_slice x1, local copies, waits for them, and re-layouts, local_reduced(): lax.dynamic_slice_in_dim(layers[0], (1 - along) * half_columns, half_colu...  2.1 us
  transfers between devices with their start and end apart: 2, of which 0 were waited for; matrix products, arithmetic and copies ran while one was open for 18% of the time, Pallas kernels for 0%

profile of v3, /device:TPU:0, one launch (start us, length us, event | category | flops | bytes accessed | tf_op | source)
XLA Modules:
  0.0 76.3 jit_solution(9726598289211294564)
XLA Ops:
  0.0 2.1 %dynamic-slice_bitcast_fusion = (bf16[2048,128]{1,0:T(8,128)(2,1)S(1)}, bf16[2048,128]{1,0:T(8,128)(2,1)}) fusion(bf16[1,2048,256]{2,1,0:T(8,128)(2,1)} %param.7, s32[]{:T(128)S(6)} %select_n.26, s32[]{:T(128)S(6)} %select_n.25), kind=kLoop, calls=%fused_computation | loop fusion | bytes 2097160 | tf_op jit(solution)/shard_map/dynamic_slice | solution.py:401
  2.1 3.0 %collective-permute-start = (bf16[2048,128]{1,0:T(8,128)(2,1)S(1)}, bf16[2048,128]{1,0:T(8,128)(2,1)S(1)}, u32[]{:S(2)}, u32[]{:S(2)}) collective-permute-start(bf16[2048,128]{1,0:T(8,128)(2,1)S(1)} %get-tuple-element.5), channel_id=1, source_target_pairs={{0,2},{2,0},{1,3},{3,1},{4,6},{6,4},{5,7},{7,5},{8,10},{10,8},{9,1... | collective-permute-start | bytes 1572872 | tf_op jit(solution)/shard_map/ppermute | solution.py:402
  5.1 0.7 fusion
  5.8 0.7 fusion.1
  6.4 0.1 collective-permute-start.1
  6.5 1.9 %copy.8.table_ref = bf16[16,128,64]{2,1,0:T(8,128)(2,1)} copy(bf16[16,128,64]{1,2,0:T(8,128)(2,1)} %param.8) | data formatting | bytes 524288 | tf_op args[1]
  8.4 9.8 %copy.9.fitting_ref = bf16[2048,1650]{1,0:T(8,128)(2,1)} copy(bf16[2048,1650]{0,1:T(8,128)(2,1)} %param.9) | data formatting | bytes 13516800 | tf_op args[2]
  18.2 0.0 collective-permute-done.1
  18.2 0.6 pad_add_fusion.meta_ref
  18.8 0.0 collective-permute-done.got_ref
  18.8 0.0 copy-start
  18.8 0.8 %copy-done = bf16[2048,128]{1,0:T(8,128)(2,1)} copy-done((bf16[2048,128]{1,0:T(8,128)(2,1)}, bf16[2048,128]{1,0:T(8,128)(2,1)S(1)}, u32[]{:S(2)}) %copy-start) | copy-done | bytes 524312
  19.6 5.4 %shard_map.73 = bf16[64,128,128]{2,1,0:T(8,128)(2,1)} custom-call(bf16[2048,128]{1,0:T(8,128)(2,1)} %get-tuple-element.6.own_ref, bf16[2048,128]{1,0:T(8,128)(2,1)} %copy-done, bf16[16,128,64]{2,1,0:T(8,128)(2,1)} %copy.8.table_ref, s32[2,3,32]{2,1,0:T(4,128)} %pad_add_fusion.meta_ref), custom_call_target="tpu_custom_call" | custom-call | tf_op jit(solution)/shard_map/pallas_call | solution.py:404
  25.0 49.7 %shard_map.74 = bf16[64,1650]{1,0:T(8,128)(2,1)} custom-call(bf16[2,4,1024,128]{3,2,1,0:T(8,128)(2,1)} %bitcast.12, bf16[2048,1650]{1,0:T(8,128)(2,1)} %copy.9.fitting_ref), custom_call_target="tpu_custom_call" | custom-call | tf_op jit(solution)/shard_map/pallas_call | solution.py:353
  74.7 1.6 %copy.11 = bf16[64,1650]{1,0:T(8,128)(2,1)} copy(bf16[64,1650]{1,0:T(8,128)(2,1)} %shard_map.74) | data formatting | bytes 422400
Async XLA Ops:
  2.1 16.7 %collective-permute-start = (bf16[2048,128]{1,0:T(8,128)(2,1)S(1)}, bf16[2048,128]{1,0:T(8,128)(2,1)S(1)}, u32[]{:S(2)}, u32[]{:S(2)}) collective-permute-start(bf16[2048,128]{1,0:T(8,128)(2,1)S(1)} %get-tuple-element.5), channel_id=1, source_target_pairs={{0,2},{2,0},{1,3},{3,1},{4,6},{6,4},{5,7},{7,5},{8,10},{10,8},{9,1... | collective-permute-start | bytes 1572872 | tf_op jit(solution)/shard_map/ppermute | solution.py:402
  6.4 11.8 %collective-permute-start.1 = (s32[3,32]{1,0:T(4,128)S(1)}, s32[3,32]{1,0:T(4,128)S(1)}, u32[]{:S(2)}, u32[]{:S(2)}) collective-permute-start(s32[3,32]{1,0:T(4,128)S(1)} %get-tuple-element.8), channel_id=1, source_target_pairs={{0,2},{2,0},{1,3},{3,1},{4,6},{6,4},{5,7},{7,5},{8,10},{10,8},{9,1... | collective-permute-start | bytes 1160 | tf_op jit(solution)/shard_map/ppermute | solution.py:403
  18.8 0.8 %copy-start = (bf16[2048,128]{1,0:T(8,128)(2,1)}, bf16[2048,128]{1,0:T(8,128)(2,1)S(1)}, u32[]{:S(2)}) copy-start(bf16[2048,128]{1,0:T(8,128)(2,1)S(1)} %collective-permute-done.got_ref) | copy-start | bytes 1572868

commit v4 on v3

--- a/solution.py
+++ b/solution.py
@@ -64,27 +64,85 @@
     ).astype(jnp.bfloat16)
 
 
-def terms_kernel(own_ref, got_ref, table_ref, meta_ref, out_ref, total_ref):
-    entries = meta_ref.shape[2]
+def swap_kernel(
+    rows_ref, meta_ref, turned_ref, got_ref, got_meta_ref, table_ref, send_sem, recv_sem
+):
+    me = lax.axis_index("layer")
+    half = got_ref.shape[1]
+    partner = lax.rem(me + 2, 4)
+    barrier = pltpu.get_barrier_semaphore()
+    pl.semaphore_signal(barrier, inc=1, device_id={"layer": partner}, device_id_type=MESH)
+    pl.semaphore_wait(barrier, 1)
+    first = pl.multiple_of((1 - me // 2) * half, half)
+    copies = [
+        pltpu.make_async_remote_copy(
+            src_ref=source,
+            dst_ref=target,
+            send_sem=send_sem.at[index],
+            recv_sem=recv_sem.at[index],
+            device_id={"layer": partner},
+            device_id_type=MESH,
+        )
+        for index, (source, target) in enumerate(
+            ((meta_ref, got_meta_ref), (rows_ref.at[:, pl.ds(first, half)], got_ref))
+        )
+    ]
+    for copy in copies:
+        copy.start()
+    for index in range(table_ref.shape[0]):
+        table_ref[index] = turned_ref[index].T
+    for copy in copies:
+        copy.wait()
+
+
+def swap(rows, meta, table):
+    any_space = pl.BlockSpec(memory_space=pl.ANY)
+    vmem = pl.BlockSpec(memory_space=pltpu.VMEM)
+    return pl.pallas_call(
+        swap_kernel,
+        out_shape=(
+            jax.ShapeDtypeStruct((rows.shape[0], rows.shape[1] // 2), rows.dtype),
+            jax.ShapeDtypeStruct(meta.shape, meta.dtype),
+            jax.ShapeDtypeStruct(table.shape, table.dtype),
+        ),
+        in_specs=[any_space, any_space, vmem],
+        out_specs=(any_space, any_space, vmem),
+        scratch_shapes=[pltpu.SemaphoreType.DMA((2,)), pltpu.SemaphoreType.DMA((2,))],
+        compiler_params=pltpu.CompilerParams(collective_id=1, has_side_effects=True),
+    )(rows, meta, table.transpose(0, 2, 1))
+
+
+def terms_kernel(
+    peers, half_slices, own_ref, got_ref, table_ref, meta_ref, got_meta_ref, out_ref, total_ref
+):
+    entries = meta_ref.shape[1]
     block_rows = table_ref.shape[2]
+    half = got_ref.shape[1]
+    first = pl.multiple_of(lax.axis_index("layer") // 2 * half, half)
     total_ref[...] = jnp.zeros_like(total_ref)
     group = 8 if entries % 8 == 0 else 1
-    for part, rows_ref in enumerate((own_ref, got_ref)):
+    for index_ref, rows_ref, lanes in (
+        (meta_ref, own_ref, pl.ds(first, half)),
+        (got_meta_ref, got_ref, slice(None)),
+    ):
 
         def step(index, carry):
             terms = []
             for offset in range(group):
                 entry = index * group + offset
-                start = pl.multiple_of(meta_ref[part, 1, entry] * block_rows, block_rows)
+                start = pl.multiple_of(index_ref[2, entry] * block_rows, block_rows)
                 terms.append(
                     jnp.dot(
-                        table_ref[meta_ref[part, 2, entry]],
-                        rows_ref[pl.ds(start, block_rows), :],
+                        table_ref[index_ref[3, entry]],
+                        rows_ref[pl.ds(start, block_rows), lanes],
                         preferred_element_type=jnp.float32,
                     )
                 )
             for offset in range(group):
-                place = meta_ref[part, 0, index * group + offset]
+                entry = index * group + offset
+                local_now = index_ref[1, entry]
+                upper = (local_now >= half_slices).astype(jnp.int32)
+                place = (upper * (peers - 1) + index_ref[0, entry]) * half_slices + local_now
                 total_ref[place] += terms[offset]
             return carry
 
@@ -108,7 +166,7 @@
     steps = core_send.shape[0]
     piece_rows = pieces.shape[1]
     rows = piece_rows // steps
-    width = fit.shape[1]
+    width = fit.shape[0]
     half_columns = pieces.shape[2]
     out_rows = out_ref.shape[0]
     mate = row + 1 - 2 * lax.rem(row, 2)
@@ -191,8 +249,8 @@
                 first = half * piece_rows + step * rows
                 term = lax.dot_general(
                     left,
-                    fit[first : first + rows, start:stop],
-                    (((0,), (0,)), ((), ())),
+                    fit[start:stop, first : first + rows],
+                    (((0,), (1,)), ((), ())),
                     preferred_element_type=jnp.float32,
                 )
                 value = term if value is None else value + term
@@ -356,7 +414,7 @@
         in_specs=[pl.BlockSpec(memory_space=pltpu.VMEM), pl.BlockSpec(memory_space=pl.ANY)],
         out_specs=pl.BlockSpec(memory_space=pltpu.VMEM),
         scratch_shapes=[
-            pltpu.VMEM((depth, width), jnp.bfloat16),
+            pltpu.VMEM((width, depth), jnp.bfloat16),
             pltpu.VMEM((peers, piece_rows, half_columns), jnp.bfloat16),
             pltpu.VMEM((peers, piece_rows, half_columns), jnp.bfloat16),
             pltpu.VMEM((4, piece_rows, half_columns), jnp.bfloat16),
@@ -375,7 +433,7 @@
             dma((4, 3)),
         ],
         compiler_params=pltpu.CompilerParams(collective_id=0, has_side_effects=True),
-    )(partial, fitting)
+    )(partial, fitting.T)
 
 
 def local_reduced(layers, table, fitting, owner, local_slice, block_index, weight_index):
@@ -386,29 +444,16 @@
     half_slices = owned_slices // 2
     half_columns = columns // 2
     slice_total = peer_count * owned_slices
-    me = lax.axis_index("layer")
-    along = me // 2
-    swap_x = [(0, 2), (2, 0), (1, 3), (3, 1)]
-
-    local_now = local_slice[0]
-    place = (
-        (local_now // half_slices) * (peer_count * half_slices)
-        + owner[0, :, 0] * half_slices
-        + local_now % half_slices
-    )
-    meta = jnp.stack([place, block_index[0], weight_index[0]])
-    own = lax.dynamic_slice_in_dim(layers[0], along * half_columns, half_columns, 1)
-    other = lax.dynamic_slice_in_dim(layers[0], (1 - along) * half_columns, half_columns, 1)
-    got = lax.ppermute(other, "layer", swap_x)
-    got_meta = lax.ppermute(meta, "layer", swap_x)
+    meta = jnp.stack([owner[0, :, 0], local_slice[0], block_index[0], weight_index[0]])
+    got, got_meta, turned = swap(layers[0], meta, table)
     partial = pl.pallas_call(
-        terms_kernel,
+        functools.partial(terms_kernel, peer_count, half_slices),
         out_shape=jax.ShapeDtypeStruct((slice_total, slice_rows, half_columns), jnp.bfloat16),
         in_specs=[pl.BlockSpec(memory_space=pltpu.VMEM)] * 3
-        + [pl.BlockSpec(memory_space=pltpu.SMEM)],
+        + [pl.BlockSpec(memory_space=pltpu.SMEM)] * 2,
         out_specs=pl.BlockSpec(memory_space=pltpu.VMEM),
         scratch_shapes=[pltpu.VMEM((slice_total, slice_rows, half_columns), jnp.float32)],
-    )(own, got, table, jnp.stack([meta, got_meta]))
+    )(layers[0], got, turned, meta, got_meta)
     partial = partial.reshape(2, peer_count, half_slices * slice_rows, half_columns)
     return exchange(partial, fitting)
 

time: 76.8 us -> 75.1 us (0.978)
  Pallas kernels: 55.1 us -> 72 us
  local copies, waits for them, and re-layouts: 16.2 us -> 1.63 us
  starting transfers between devices: 3.02 us -> 0 us
    pallas_call x1 -> x2, Pallas kernels: 5.36 us -> 22.5 us  [the longest x1 17 us: swap(): pl.pallas_call(swap_kernel, out_shape=(jax.ShapeDtypeStruct((rows.shape[0...]
    unnamed x5 -> x1, local copies, waits for them, and re-layouts: 14.1 us -> 1.63 us
    ppermute x2 -> x0, starting transfers between devices: 3.02 us -> none  [the longest x1 2.97 us: local_reduced(): got = lax.ppermute(other, 'layer', swap_x)]
    dynamic_slice x1 -> x0, local copies, waits for them, and re-layouts: 2.1 us -> none  [local_reduced(): lax.dynamic_slice_in_dim(layers[0], (1 - along) * half_columns, half_colu...]
  transfers between devices with their start and end apart: 2 -> 0, of which waited for: 0 -> 0; matrix products, arithmetic and copies ran while one was open for 18% -> 0% of each run, Pallas kernels for 0% -> 0%
where the time goes in v4:
time: 75.1 us; the launch traced here: 74.9 us
  Pallas kernels  72 us (96%)
  local copies, waits for them, and re-layouts  1.63 us (2%)
  other arithmetic  1.29 us (2%)
    pallas_call x1, Pallas kernels, exchange(): pl.pallas_call(functools.partial(exchange_kernel, peers), out_shape=jax.S...  49.4 us
    pallas_call x1, Pallas kernels, swap(): pl.pallas_call(swap_kernel, out_shape=(jax.ShapeDtypeStruct((rows.shape[0...  17 us
    pallas_call x1, Pallas kernels, local_reduced(): pl.pallas_call(functools.partial(terms_kernel, peer_count, half_slices),...  5.47 us
    unnamed x1, local copies, waits for them, and re-layouts  1.63 us

profile of v4, /device:TPU:0, one launch (start us, length us, event | category | flops | bytes accessed | tf_op | source)
XLA Modules:
  0.0 74.9 jit_solution(10339732319125682468)
XLA Ops:
  0.0 1.3 %pad_add_fusion.meta_ref = s32[4,32]{1,0:T(4,128)} fusion(s32[1,32]{1,0:T(1,128)} %param.13, s32[1,32]{1,0:T(1,128)} %param.12, s32[1,32]{1,0:T(1,128)} %param.11, s32[1,32]{1,0:T(1,128)} %bitcast.10), kind=kLoop, calls=%fused_computation | loop fusion | flops 384 | bytes 1024 | tf_op jit(solution)/shard_map/stack | solution.py:447
  1.3 17.0 %shard_map.73 = (bf16[2048,128]{1,0:T(8,128)(2,1)}, s32[4,32]{1,0:T(4,128)}, bf16[16,128,64]{2,1,0:T(8,128)(2,1)}) custom-call(bf16[2048,256]{1,0:T(8,128)(2,1)} %bitcast.7, s32[4,32]{1,0:T(4,128)} %pad_add_fusion.meta_ref, bf16[16,64,128]{2,1,0:T(8,128)(2,1)} %bitcast.9), custom_call_target="tpu_custom_call" | custom-call | tf_op jit(solution)/shard_map/pallas_call | solution.py:101
  18.3 5.5 %shard_map.74 = bf16[64,128,128]{2,1,0:T(8,128)(2,1)} custom-call(bf16[2048,256]{1,0:T(8,128)(2,1)} %bitcast.8, bf16[2048,128]{1,0:T(8,128)(2,1)} %get-tuple-element.8.got_ref, bf16[16,128,64]{2,1,0:T(8,128)(2,1)} %get-tuple-element.9.table_ref, s32[4,32]{1,0:T(4,128)} %pad_add_fusion.meta_ref, s32[4,32]{1,0:T(4,128)} %get-tuple-element.10.got_meta_ref), custom_call_target="tpu_custom_call" | custom-call | tf_op jit(solution)/shard_map/pallas_call | solution.py:449
  23.8 49.4 %shard_map.75 = bf16[64,1650]{1,0:T(8,128)(2,1)} custom-call(bf16[2,4,1024,128]{3,2,1,0:T(8,128)(2,1)} %bitcast.5, bf16[1650,2048]{1,0:T(8,128)(2,1)} %bitcast.6), custom_call_target="tpu_custom_call" | custom-call | tf_op jit(solution)/shard_map/pallas_call | solution.py:411
  73.3 1.6 %copy.9 = bf16[64,1650]{1,0:T(8,128)(2,1)} copy(bf16[64,1650]{1,0:T(8,128)(2,1)} %shard_map.75) | data formatting | bytes 422400

commit v5 on v4

--- a/solution.py
+++ b/solution.py
@@ -120,7 +120,7 @@
     half = got_ref.shape[1]
     first = pl.multiple_of(lax.axis_index("layer") // 2 * half, half)
     total_ref[...] = jnp.zeros_like(total_ref)
-    group = 8 if entries % 8 == 0 else 1
+    group = 16 if entries % 16 == 0 else 1
     for index_ref, rows_ref, lanes in (
         (meta_ref, own_ref, pl.ds(first, half)),
         (got_meta_ref, got_ref, slice(None)),
@@ -152,7 +152,7 @@
         out_ref[index] = total_ref[index].astype(out_ref.dtype)
         return carry
 
-    lax.fori_loop(0, out_ref.shape[0], write, 0)
+    lax.fori_loop(0, out_ref.shape[0], write, 0, unroll=4)
 
 
 def exchange_kernel(

time: 75.1 us -> 74.3 us (0.989)
  Pallas kernels: 72 us -> 71.1 us
    pallas_call x1, Pallas kernels: 5.47 us -> 4.61 us  [local_reduced(): pl.pallas_call(functools.partial(terms_kernel, peer_count, half_slices),...]
where the time goes in v5:
time: 74.3 us; the launch traced here: 74 us
  Pallas kernels  71.1 us (96%)
  local copies, waits for them, and re-layouts  1.63 us (2%)
  other arithmetic  1.29 us (2%)
    pallas_call x1, Pallas kernels, exchange(): pl.pallas_call(functools.partial(exchange_kernel, peers), out_shape=jax.S...  49.4 us
    pallas_call x1, Pallas kernels, swap(): pl.pallas_call(swap_kernel, out_shape=(jax.ShapeDtypeStruct((rows.shape[0...  17 us
    pallas_call x1, Pallas kernels, local_reduced(): pl.pallas_call(functools.partial(terms_kernel, peer_count, half_slices),...  4.61 us
    unnamed x1, local copies, waits for them, and re-layouts  1.63 us

profile of v5, /device:TPU:0, one launch (start us, length us, event | category | flops | bytes accessed | tf_op | source)
XLA Modules:
  0.0 74.0 jit_solution(12650870593379600485)
XLA Ops:
  0.0 1.3 %pad_add_fusion.meta_ref = s32[4,32]{1,0:T(4,128)} fusion(s32[1,32]{1,0:T(1,128)} %param.13, s32[1,32]{1,0:T(1,128)} %param.12, s32[1,32]{1,0:T(1,128)} %param.11, s32[1,32]{1,0:T(1,128)} %bitcast.10), kind=kLoop, calls=%fused_computation | loop fusion | flops 384 | bytes 1024 | tf_op jit(solution)/shard_map/stack | solution.py:447
  1.3 17.0 %shard_map.73 = (bf16[2048,128]{1,0:T(8,128)(2,1)}, s32[4,32]{1,0:T(4,128)}, bf16[16,128,64]{2,1,0:T(8,128)(2,1)}) custom-call(bf16[2048,256]{1,0:T(8,128)(2,1)} %bitcast.7, s32[4,32]{1,0:T(4,128)} %pad_add_fusion.meta_ref, bf16[16,64,128]{2,1,0:T(8,128)(2,1)} %bitcast.9), custom_call_target="tpu_custom_call" | custom-call | tf_op jit(solution)/shard_map/pallas_call | solution.py:101
  18.3 4.6 %shard_map.74 = bf16[64,128,128]{2,1,0:T(8,128)(2,1)} custom-call(bf16[2048,256]{1,0:T(8,128)(2,1)} %bitcast.8, bf16[2048,128]{1,0:T(8,128)(2,1)} %get-tuple-element.8.got_ref, bf16[16,128,64]{2,1,0:T(8,128)(2,1)} %get-tuple-element.9.table_ref, s32[4,32]{1,0:T(4,128)} %pad_add_fusion.meta_ref, s32[4,32]{1,0:T(4,128)} %get-tuple-element.10.got_meta_ref), custom_call_target="tpu_custom_call" | custom-call | tf_op jit(solution)/shard_map/pallas_call | solution.py:449
  23.0 49.4 %shard_map.75 = bf16[64,1650]{1,0:T(8,128)(2,1)} custom-call(bf16[2,4,1024,128]{3,2,1,0:T(8,128)(2,1)} %bitcast.5, bf16[1650,2048]{1,0:T(8,128)(2,1)} %bitcast.6), custom_call_target="tpu_custom_call" | custom-call | tf_op jit(solution)/shard_map/pallas_call | solution.py:411
  72.4 1.6 %copy.9 = bf16[64,1650]{1,0:T(8,128)(2,1)} copy(bf16[64,1650]{1,0:T(8,128)(2,1)} %shard_map.75) | data formatting | bytes 422400

commit v6 on v5

--- a/solution.py
+++ b/solution.py
@@ -157,8 +157,8 @@
 
 def exchange_kernel(
     peers, part_ref, fitting_ref, out_ref,
-    fit, core_in, both, row_in, pieces, total, product, landed,
-    fit_sem, core_send, core_recv, row_send, row_recv, layer_send, layer_recv, end_send, end_recv,
+    fit, kept, core_in, both, row_in, pieces, total, product, landed,
+    fit_sem, kept_sem, core_send, core_recv, row_send, row_recv, layer_send, layer_recv, end_send, end_recv,
 ):
     row = lax.axis_index("row")
     me = lax.axis_index("layer")
@@ -176,6 +176,8 @@
     is_middle = jnp.logical_not(is_end)
     layer_peers = [lax.rem(me + k, 4) for k in range(1, 4)]
 
+    kept_copy = pltpu.make_async_copy(part_ref.at[core], kept, kept_sem)
+    kept_copy.start()
     fit_copy = pltpu.make_async_copy(fitting_ref, fit, fit_sem)
     fit_copy.start()
     barrier = pltpu.get_barrier_semaphore()
@@ -211,9 +213,11 @@
 
     for step in range(steps):
         part = slice(step * rows, (step + 1) * rows)
+        if step == 0:
+            kept_copy.wait()
         core_copies[step].wait_recv()
         both[:, part, :] = (
-            part_ref[core, :, part, :].astype(jnp.float32) + core_in[:, part, :].astype(jnp.float32)
+            kept[:, part, :].astype(jnp.float32) + core_in[:, part, :].astype(jnp.float32)
         ).astype(both.dtype)
 
         @pl.when(is_end)
@@ -411,10 +415,11 @@
     return pl.pallas_call(
         functools.partial(exchange_kernel, peers),
         out_shape=jax.ShapeDtypeStruct((out_rows, width), jnp.bfloat16),
-        in_specs=[pl.BlockSpec(memory_space=pltpu.VMEM), pl.BlockSpec(memory_space=pl.ANY)],
+        in_specs=[pl.BlockSpec(memory_space=pl.ANY), pl.BlockSpec(memory_space=pl.ANY)],
         out_specs=pl.BlockSpec(memory_space=pltpu.VMEM),
         scratch_shapes=[
             pltpu.VMEM((width, depth), jnp.bfloat16),
+            pltpu.VMEM((peers, piece_rows, half_columns), jnp.bfloat16),
             pltpu.VMEM((peers, piece_rows, half_columns), jnp.bfloat16),
             pltpu.VMEM((peers, piece_rows, half_columns), jnp.bfloat16),
             pltpu.VMEM((4, piece_rows, half_columns), jnp.bfloat16),
@@ -422,6 +427,7 @@
             pltpu.VMEM((columns, width), jnp.float32),
             pltpu.VMEM((peers, out_rows, padded), jnp.bfloat16),
             pltpu.VMEM((4, out_rows, padded), jnp.bfloat16),
+            dma,
             dma,
             dma((steps,)),
             dma((steps,)),

time: 74.3 us -> 74.8 us (level)
  no operation moved by 1% of the time
where the time goes in v6:
time: 74.8 us; the launch traced here: 74.5 us
  Pallas kernels  71.6 us (96%)
  local copies, waits for them, and re-layouts  1.63 us (2%)
  other arithmetic  1.29 us (2%)
    pallas_call x1, Pallas kernels, exchange(): pl.pallas_call(functools.partial(exchange_kernel, peers), out_shape=jax.S...  50 us
    pallas_call x1, Pallas kernels, swap(): pl.pallas_call(swap_kernel, out_shape=(jax.ShapeDtypeStruct((rows.shape[0...  17 us
    pallas_call x1, Pallas kernels, local_reduced(): pl.pallas_call(functools.partial(terms_kernel, peer_count, half_slices),...  4.61 us
    unnamed x1, local copies, waits for them, and re-layouts  1.63 us

profile of v6, /device:TPU:0, one launch (start us, length us, event | category | flops | bytes accessed | tf_op | source)
XLA Modules:
  0.0 74.5 jit_solution(9207832313854157719)
XLA Ops:
  0.0 1.3 %pad_add_fusion.meta_ref = s32[4,32]{1,0:T(4,128)} fusion(s32[1,32]{1,0:T(1,128)} %param.13, s32[1,32]{1,0:T(1,128)} %param.12, s32[1,32]{1,0:T(1,128)} %param.11, s32[1,32]{1,0:T(1,128)} %bitcast.10), kind=kLoop, calls=%fused_computation | loop fusion | flops 384 | bytes 1024 | tf_op jit(solution)/shard_map/stack | solution.py:453
  1.3 17.0 %shard_map.73 = (bf16[2048,128]{1,0:T(8,128)(2,1)}, s32[4,32]{1,0:T(4,128)}, bf16[16,128,64]{2,1,0:T(8,128)(2,1)}) custom-call(bf16[2048,256]{1,0:T(8,128)(2,1)} %bitcast.7, s32[4,32]{1,0:T(4,128)} %pad_add_fusion.meta_ref, bf16[16,64,128]{2,1,0:T(8,128)(2,1)} %bitcast.9), custom_call_target="tpu_custom_call" | custom-call | tf_op jit(solution)/shard_map/pallas_call | solution.py:101
  18.3 4.6 %shard_map.74 = bf16[64,128,128]{2,1,0:T(8,128)(2,1)} custom-call(bf16[2048,256]{1,0:T(8,128)(2,1)} %bitcast.8, bf16[2048,128]{1,0:T(8,128)(2,1)} %get-tuple-element.8.got_ref, bf16[16,128,64]{2,1,0:T(8,128)(2,1)} %get-tuple-element.9.table_ref, s32[4,32]{1,0:T(4,128)} %pad_add_fusion.meta_ref, s32[4,32]{1,0:T(4,128)} %get-tuple-element.10.got_meta_ref), custom_call_target="tpu_custom_call" | custom-call | tf_op jit(solution)/shard_map/pallas_call | solution.py:455
  23.0 50.0 %shard_map.75 = bf16[64,1650]{1,0:T(8,128)(2,1)} custom-call(bf16[2,4,1024,128]{3,2,1,0:T(8,128)(2,1)} %bitcast.5, bf16[1650,2048]{1,0:T(8,128)(2,1)} %bitcast.6), custom_call_target="tpu_custom_call" | custom-call | tf_op jit(solution)/shard_map/pallas_call | solution.py:415
  72.9 1.6 %copy.9 = bf16[64,1650]{1,0:T(8,128)(2,1)} copy(bf16[64,1650]{1,0:T(8,128)(2,1)} %shard_map.75) | data formatting | bytes 422400
